TPU v7x, 256 devices: a whole 4x4x8 slice. The times are simulated.
256 devices in a mesh: seq: 64 (over z, y, core), ch: 4 (over x).
Axes of the slice: x: 4, y: 4, z: 8, core: 2. Of those that a mesh axis runs over, the one named last changes fastest.
Arguments:
- query_proj: bfloat16 [8192, 2048], P('seq', 'ch'), may hold values from -6 to 6
- key_proj: bfloat16 [8192, 2048], P('seq', 'ch'), may hold values from -6 to 6
- value_proj: bfloat16 [8192, 2048], P('seq', 'ch'), may hold values from -6 to 6
- short_filter: float32 [3, 3, 2048], P(None, None, 'ch'), may hold values from -3.5 to 3.5
- long_filter: float32 [8192, 2048], P('seq', 'ch'), may hold values from -0.0625 to 0.0625
- skip_gain: float32 [2048], P('ch'), may hold values from 0.5 to 1.5
- out_weight: bfloat16 [2048, 4096], P('ch'), may hold values from -0.125 to 0.125
- cotangent: bfloat16 [8192, 4096], P('seq', 'ch'), may hold values from -16 to 16
Outputs:
- layer_out: bfloat16 [8192, 4096], P('seq', 'ch')
- grad_query: float32 [8192, 2048], P('seq', 'ch')
- grad_key: float32 [8192, 2048], P('seq', 'ch')
- grad_value: float32 [8192, 2048], P('seq', 'ch')
- grad_short: float32 [3, 3, 2048], P(None, None, 'ch')
- grad_filter: float32 [8192, 2048], P('seq', 'ch')
- grad_skip: float32 [2048], P('ch')
- grad_w_out_t: float32 [4096, 2048], P('seq', 'ch')
All inputs are finite; a program needn't handle non-finite values.
Results may differ from a plain program's by a relative error of at most 0.011.
Values may be sent and summed in bfloat16 or wider, within the bound.
A program may use at most 128 MiB of HBM per device.

v0:
```python
import math
import jax
import jax.numpy as jnp
from jax import lax
from jax.sharding import PartitionSpec as P

exact_mode = lax.Precision.HIGHEST


def from_behind(shard, axis, by):
    size = lax.axis_size(axis)
    pairs = [(i, i + by) for i in range(size) if 0 <= i + by < size]
    return lax.ppermute(shard, axis, pairs)


def as_sent(shard):

    def short(part):
        return part.astype(jnp.bfloat16) if part.dtype == jnp.float32 else part

    return jax.tree.map(short, shard)


def split_lanes(merged, lanes):
    return tuple(
        (merged[..., start : start + lanes] for start in range(0, merged.shape[-1], lanes))
    )


def tables(rows_out, cols_in, period):
    row_index = lax.broadcasted_iota(jnp.int32, (rows_out, cols_in), 0)
    col_index = lax.broadcasted_iota(jnp.int32, (rows_out, cols_in), 1)
    phase_angle = (row_index * col_index % period).astype(jnp.float32) * (2.0 * math.pi / period)
    return (jnp.cos(phase_angle), jnp.sin(phase_angle))


def along_rows(factor, values):
    return jnp.tensordot(factor, values, axes=1, precision=exact_mode)


def rows_spectrum(signal, basis_pair):
    return (along_rows(basis_pair[0], signal), -along_rows(basis_pair[1], signal))


def rows_inverse(complex_pair, basis_pair):
    total = along_rows(basis_pair[0], complex_pair[0]) - along_rows(basis_pair[1], complex_pair[1])
    return total / basis_pair[0].shape[1]


def block_forward(complex_pair, basis_pair):
    cosine_part, sine_part = basis_pair
    real_part = along_rows(cosine_part, complex_pair[0]) + along_rows(sine_part, complex_pair[1])
    imag_part = along_rows(cosine_part, complex_pair[1]) - along_rows(sine_part, complex_pair[0])
    return (real_part, imag_part)


def block_inverse(complex_pair, basis_pair):
    cosine_part, sine_part = basis_pair
    norming = 1.0 / cosine_part.shape[1]
    real_part = along_rows(cosine_part, complex_pair[0]) - along_rows(sine_part, complex_pair[1])
    imag_part = along_rows(cosine_part, complex_pair[1]) + along_rows(sine_part, complex_pair[0])
    return (real_part * norming, imag_part * norming)


def complex_product(first_pair, second_pair):
    return (
        first_pair[0] * second_pair[0] - first_pair[1] * second_pair[1],
        first_pair[0] * second_pair[1] + first_pair[1] * second_pair[0],
    )


def conj_product(first_pair, second_pair):
    return (
        first_pair[0] * second_pair[0] + first_pair[1] * second_pair[1],
        first_pair[0] * second_pair[1] - first_pair[1] * second_pair[0],
    )


def on_device(
    query_proj, key_proj, value_proj, short_filter, long_filter, skip_gain, out_weight, cotangent
):
    block_rows = query_proj.shape[0]
    tap_count = short_filter.shape[1]
    block_count = lax.axis_size("seq")
    streams = jnp.stack([query_proj, key_proj, value_proj])
    earlier = from_behind(streams[:, block_rows - (tap_count - 1) :], "seq", 1)
    extended = jnp.concatenate([earlier, streams], axis=1).astype(jnp.float32)
    shifted = [
        extended[:, tap_count - 1 - offset : tap_count - 1 - offset + block_rows]
        for offset in range(tap_count)
    ]
    filtered = sum(
        (short_filter[:, offset][:, None, :] * shifted[offset] for offset in range(tap_count))
    )
    query_short, key_short, value_short = (filtered[0], filtered[1], filtered[2])
    product = key_short * value_short
    forward_basis = tables(2 * block_rows, block_rows, 2 * block_rows)
    full_basis = tables(2 * block_rows, 2 * block_rows, 2 * block_rows)
    half_basis = tables(block_rows, 2 * block_rows, 2 * block_rows)
    block_basis = tables(2 * block_count, block_count, 2 * block_count)
    return_basis = tables(block_count, 2 * block_count, 2 * block_count)
    input_pair = rows_spectrum(product, forward_basis)
    filter_pair = rows_spectrum(long_filter, forward_basis)
    lanes = product.shape[1]
    moved_data = split_lanes(
        lax.all_to_all(
            jnp.concatenate([input_pair[0], input_pair[1], filter_pair[0], filter_pair[1]], axis=1)[
                None
            ],
            "seq",
            split_axis=1,
            concat_axis=0,
            tiled=True,
        ),
        lanes,
    )
    input_spectrum = block_forward((moved_data[0], moved_data[1]), block_basis)
    filter_spectrum = block_forward((moved_data[2], moved_data[3]), block_basis)
    inverse_pair = block_inverse(complex_product(filter_spectrum, input_spectrum), return_basis)
    returned = split_lanes(
        lax.all_to_all(
            jnp.concatenate(inverse_pair, axis=-1), "seq", split_axis=0, concat_axis=1, tiled=True
        ),
        lanes,
    )
    folded = rows_inverse((returned[0][0], returned[1][0]), full_basis)
    carried = from_behind(folded[block_rows:], "seq", 1)
    convolved = folded[:block_rows] + carried
    mixed_seq = convolved + skip_gain * product
    gated_values = (query_short * mixed_seq).astype(jnp.bfloat16)
    partial_value = jnp.dot(gated_values, out_weight, preferred_element_type=jnp.float32)
    layer_out = lax.psum_scatter(partial_value, "ch", scatter_dimension=1, tiled=True).astype(
        jnp.bfloat16
    )
    full_cotangent = lax.all_gather(cotangent, "ch", axis=1, tiled=True)
    grad_gated = lax.dot_general(
        full_cotangent, out_weight, (((1,), (1,)), ((), ())), preferred_element_type=jnp.float32
    )
    weight_terms = lax.dot_general(
        full_cotangent, gated_values, (((0,), (0,)), ((), ())), preferred_element_type=jnp.float32
    )
    grad_mixed = grad_gated * query_short
    grad_query_short = grad_gated * mixed_seq
    following = from_behind(grad_mixed.astype(jnp.bfloat16), "seq", -1).astype(grad_mixed.dtype)
    spread = jnp.concatenate([grad_mixed, following], axis=0)
    grad_pair = rows_spectrum(spread, full_basis)
    moved_grad = split_lanes(
        lax.all_to_all(
            jnp.concatenate(grad_pair, axis=1)[None].astype(jnp.bfloat16),
            "seq",
            split_axis=1,
            concat_axis=0,
            tiled=True,
        ).astype(jnp.float32),
        lanes,
    )
    grad_spectrum = block_forward(moved_grad, block_basis)
    input_back = block_inverse(conj_product(filter_spectrum, grad_spectrum), return_basis)
    filter_back = block_inverse(conj_product(input_spectrum, grad_spectrum), return_basis)
    returned_grad = split_lanes(
        lax.all_to_all(
            as_sent(jnp.concatenate(input_back + filter_back, axis=-1)),
            "seq",
            split_axis=0,
            concat_axis=1,
            tiled=True,
        ),
        lanes,
    )
    conv_grad = rows_inverse((returned_grad[0][0], returned_grad[1][0]), half_basis)
    grad_filter = rows_inverse((returned_grad[2][0], returned_grad[3][0]), half_basis)
    grad_product = conv_grad + skip_gain * grad_mixed
    grad_streams = jnp.stack(
        [grad_query_short, grad_product * value_short, grad_product * key_short]
    )
    later_rows = from_behind(grad_streams[:, : tap_count - 1], "seq", -1)
    padded_grad = jnp.concatenate([grad_streams, later_rows], axis=1)
    grad_inputs = sum(
        (
            short_filter[:, offset][:, None, :] * padded_grad[:, offset : offset + block_rows]
            for offset in range(tap_count)
        )
    )
    short_terms = jnp.stack(
        [jnp.sum(grad_streams * shifted[offset], axis=1) for offset in range(tap_count)], axis=1
    )
    skip_terms = jnp.sum(grad_mixed * product, axis=0)
    channel_count = skip_terms.shape[0]
    sum_rows = short_terms.shape[0] * short_terms.shape[1] + 1
    padded_rows = -(-sum_rows // 8) * 8
    small_terms = jnp.concatenate(
        [
            short_terms.reshape(sum_rows - 1, channel_count),
            skip_terms[None],
            jnp.zeros((padded_rows - sum_rows, channel_count), jnp.float32),
        ]
    )
    weight_blocks = weight_terms.reshape(block_count, -1, channel_count)
    block_height = weight_blocks.shape[1]
    combined = jnp.concatenate(
        [weight_blocks, jnp.broadcast_to(small_terms, (block_count, padded_rows, channel_count))],
        axis=1,
    )
    reduced = lax.psum_scatter(
        combined.reshape(-1, channel_count), "seq", scatter_dimension=0, tiled=True
    )
    grad_w_out_t = reduced[:block_height]
    grad_short = reduced[block_height : block_height + sum_rows - 1].reshape(short_terms.shape)
    grad_skip = reduced[block_height + sum_rows - 1]
    return (
        layer_out,
        grad_inputs[0],
        grad_inputs[1],
        grad_inputs[2],
        grad_short,
        grad_filter,
        grad_skip,
        grad_w_out_t,
    )


def solution(mesh):
    in_specs = (
        P("seq", "ch"),
        P("seq", "ch"),
        P("seq", "ch"),
        P(None, None, "ch"),
        P("seq", "ch"),
        P("ch"),
        P("ch", None),
        P("seq", "ch"),
    )
    out_specs = (
        P("seq", "ch"),
        P("seq", "ch"),
        P("seq", "ch"),
        P("seq", "ch"),
        P(None, None, "ch"),
        P("seq", "ch"),
        P("ch"),
        P("seq", "ch"),
    )
    return jax.shard_map(
        on_device, mesh=mesh, in_specs=in_specs, out_specs=out_specs, check_vma=False
    )
```

profile of v0, /device:TPU:2, one launch (start us, length us, event | category | flops | bytes accessed | tf_op | source)
XLA Modules:
  0.0 450.7 jit_solution(9208655784076676578)
XLA Ops:
  8.7 1.7 collective-permute-start
  11.3 1.1 maximum_convert_fusion
  12.7 25.7 %all-gather.2.cloned.1.call-done = bf16[128,4096]{1,0:T(8,128)(2,1)} async-done(((bf16[128,1024]{1,0:T(8,128)(2,1)}), bf16[128,4096]{1,0:T(8,128)(2,1)}) %all-gather.2.cloned.1.call-update) | async-done | bytes 1048592 | tf_op jit(solution)/shard_map/all_gather | solution.py:135
  38.4 4.8 %multiply_reduce_fusion.3 = (f32[512]{0:T(512)S(1)}, f32[128,512]{1,0:T(8,128)S(1)}, f32[128,512]{1,0:T(8,128)S(1)}, f32[128,512]{1,0:T(8,128)}) fusion(f32[3,128,512]{2,1,0:T(8,128)S(1)} %multiply_add_fusion.3, bf16[128,4096]{1,0:T(8,128)(2,1)} %all-gather.2.cloned.1.call-done, bf16[512,4096]{1,0:T(8,128)(2,1)} %param.14), kind=kOutput, calls=%fused_computation.95 | convolution fusion | flops 537132544 | bytes 6817792 | tf_op jit(solution)/shard_map/dot_general | solution.py:136
  43.2 1.3 collective-permute-start.2
  44.5 1.9 collective-permute-done.2
  46.5 1.6 fusion.12
  48.1 1.6 fusion.13
  51.1 3.7 reduce.3
  54.8 1.1 reshape.83
  56.0 13.8 %all-to-all-start.2 = ((bf16[64,2,2048]{2,1,0:T(2,128)(2,1)}), bf16[64,2,2048]{2,1,0:T(2,128)(2,1)S(1)}, u32[]{:S(2)}, u32[]{:S(2)}) async-start(bf16[64,2,2048]{2,1,0:T(2,128)(2,1)} %reshape.83), calls=%async_computation.3 | async-start | bytes 1048576 | tf_op jit(solution)/shard_map/all_to_all | solution.py:148
  69.8 1.1 convolution_negate_fusion.1
  70.9 1.0 fusion.75
  71.9 1.1 convolution_negate_fusion.2
  73.0 1.1 fusion.77
  74.2 3.5 copy.39
  77.7 9.7 %all-to-all-done.2 = bf16[64,2,2048]{2,1,0:T(2,128)(2,1)S(1)} async-done(((bf16[64,2,2048]{2,1,0:T(2,128)(2,1)}), bf16[64,2,2048]{2,1,0:T(2,128)(2,1)S(1)}, u32[]{:S(2)}, u32[]{:S(2)}) %all-to-all-start.2) | async-done | bytes 524320 | tf_op jit(solution)/shard_map/all_to_all | solution.py:148
  88.2 5.8 %all-to-all-start = ((f32[1,256,2048]{2,0,1:T(1,128)}), f32[1,256,2048]{2,0,1:T(1,128)S(1)}, u32[]{:S(2)}, u32[]{:S(2)}) async-start(f32[1,256,2048]{2,0,1:T(1,128)} %copy.39), calls=%async_computation | async-start | bytes 4194304 | tf_op jit(solution)/shard_map/all_to_all | solution.py:106
  94.0 4.8 %reshape.84 = bf16[256,1,1024]{2,1,0:T(2,128)(2,1)} reshape(bf16[64,2,2048]{2,1,0:T(2,128)(2,1)} %copy-done.13) | data formatting | bytes 1048576
  98.9 5.1 %bitcast_reduce_fusion = bf16[256,1024]{1,0:T(8,128)(2,1)} fusion(bf16[256,1,1024]{2,1,0:T(2,128)(2,1)} %reshape.84), kind=kLoop, calls=%fused_computation.345 | loop fusion | bytes 1048576 | tf_op jit(solution)/shard_map/all_to_all | solution.py:148
  104.0 2.0 all_to_all.41
  106.0 1.2 fusion.301
  108.7 1.8 convolution_add_fusion
  110.5 1.7 convolution_subtract_fusion
  112.2 33.2 %all-to-all-done = f32[1,256,2048]{2,0,1:T(1,128)S(1)} async-done(((f32[1,256,2048]{2,0,1:T(1,128)}), f32[1,256,2048]{2,0,1:T(1,128)S(1)}, u32[]{:S(2)}, u32[]{:S(2)}) %all-to-all-start) | async-done | bytes 2097184 | tf_op jit(solution)/shard_map/all_to_all | solution.py:106
  145.4 6.8 %reduce = f32[256,2048]{1,0:T(8,128)} reduce(f32[1,256,2048]{2,0,1:T(1,128)S(1)} %all-to-all-done, f32[]{:T(128)} %constant.71), dimensions={0}, to_apply=%all_to_all.16.reduce_sub_computation | reduce | bytes 4194308 | tf_op jit(solution)/shard_map/all_to_all | solution.py:106
  152.2 2.0 all_to_all.17
  154.6 1.2 fusion.24
  155.8 1.2 fusion.20
  157.0 1.2 convolution_add_fusion.1
  158.2 1.2 convolution_subtract_fusion.1
  159.4 1.2 fusion.30
  160.6 1.2 fusion.26
  161.8 1.2 convolution_add_fusion.2
  163.0 2.8 multiply_add_fusion.1
  165.8 1.6 fusion.111
  167.4 1.0 fusion.115
  171.0 1.6 copy.44
  172.6 5.6 %all-to-all-start.1 = ((f32[64,4,1024]{2,1,0:T(4,128)}), f32[64,4,1024]{2,1,0:T(4,128)}, u32[]{:S(2)}, u32[]{:S(2)}) async-start(f32[64,4,1024]{2,1,0:T(4,128)} %copy.44), calls=%async_computation.1 | async-start | bytes 2097152 | tf_op jit(solution)/shard_map/all_to_all | solution.py:121
  184.4 1.8 copy.48
  186.2 20.8 %all-to-all-done.1 = f32[64,4,1024]{2,1,0:T(4,128)} async-done(((f32[64,4,1024]{2,1,0:T(4,128)}), f32[64,4,1024]{2,1,0:T(4,128)}, u32[]{:S(2)}, u32[]{:S(2)}) %all-to-all-start.1) | async-done | bytes 1048608 | tf_op jit(solution)/shard_map/all_to_all | solution.py:121
  206.9 5.8 %all-to-all-start.3 = ((bf16[64,4,2048]{2,1,0:T(4,128)(2,1)}), bf16[64,4,2048]{2,1,0:T(4,128)(2,1)S(1)}, u32[]{:S(2)}, u32[]{:S(2)}) async-start(bf16[64,4,2048]{2,1,0:T(4,128)(2,1)} %copy.48), calls=%async_computation.4 | async-start | bytes 2097152 | tf_op jit(solution)/shard_map/all_to_all | solution.py:161
  212.8 1.6 all_to_all.19
  214.4 1.6 fusion.19
  216.0 1.6 fusion.6
  218.5 2.9 collective-permute-start.1
  221.4 20.3 %all-to-all-done.3 = bf16[64,4,2048]{2,1,0:T(4,128)(2,1)S(1)} async-done(((bf16[64,4,2048]{2,1,0:T(4,128)(2,1)}), bf16[64,4,2048]{2,1,0:T(4,128)(2,1)S(1)}, u32[]{:S(2)}, u32[]{:S(2)}) %all-to-all-start.3) | async-done | bytes 1048608 | tf_op jit(solution)/shard_map/all_to_all | solution.py:161
  241.6 1.1 all_to_all.43
  242.8 1.8 fusion.36
  244.6 1.9 fusion.16
  246.5 1.0 multiply_bitcast_fusion.2
  247.7 2.1 fusion.303
  250.0 1.4 collective-permute-start.3
  251.4 4.5 %convolution_bitcast_fusion = f32[4096,512]{0,1:T(8,128)} fusion(bf16[128,512]{1,0:T(8,128)(2,1)S(1)} %get-tuple-element.36, bf16[128,4096]{1,0:T(8,128)(2,1)S(1)} %copy-done.10), kind=kOutput, calls=%fused_computation.1 | convolution fusion | flops 536870912 | bytes 9568256 | tf_op jit(solution)/shard_map/dot_general | solution.py:139
  255.9 9.1 %copy.49 = f32[4096,512]{1,0:T(8,128)} copy(f32[4096,512]{0,1:T(8,128)} %convolution_bitcast_fusion) | data formatting | bytes 16777216 | tf_op jit(solution)/shard_map/dot_general | solution.py:139
  265.1 1.4 multiply_reduce_fusion.2
  266.9 9.7 %pad_maximum_fusion = f32[64,80,512]{2,1,0:T(8,128)} fusion(f32[64,16,512]{2,1,0:T(8,128)S(1)} %broadcast_in_dim.18, f32[64,64,512]{2,1,0:T(8,128)} %bitcast.158), kind=kLoop, calls=%fused_computation | loop fusion | flops 2621440 | bytes 20971520 | tf_op jit(solution)/shard_map/concatenate | solution.py:200
  276.6 1.2 copy-done.18
  278.6 1.5 fusion.14
  280.1 0.9 slice_bitcast_fusion.8
  281.0 1.8 convert_element_type.109
  282.8 156.7 %reduce-scatter.5.cloned.1.call-done = f32[80,512]{1,0:T(8,128)} async-done(((f32[5120,512]{1,0:T(8,128)}), f32[80,512]{1,0:T(8,128)}) %reduce-scatter.5.cloned.1.call-update) | async-done | bytes 163856 | tf_op jit(solution)/shard_map/reduce_scatter | solution.py:204
  440.8 1.6 slice.163
  442.4 1.3 slice.162
  (92 shorter events, 19.1 us)
Async XLA Ops:
  7.2 62.6 %copy-start = (f32[128,512]{1,0:T(8,128)S(1)}, f32[128,512]{1,0:T(8,128)}, u32[]{:S(2)}) copy-start(f32[128,512]{1,0:T(8,128)} %param.12) | copy-start | bytes 786436
  7.2 31.2 %all-gather.2.cloned.1.call-start = ((), (), s32[]{:S(2)}) async-start(), calls=%async_computation.7 | async-start | bytes 1310720 | tf_op jit(solution)/shard_map/all_gather | solution.py:135
  8.7 2.6 collective-permute-start
  12.7 30.4 %copy-start.6 = (f32[3,128,512]{2,1,0:T(8,128)}, f32[3,128,512]{2,1,0:T(8,128)S(1)}, u32[]{:S(2)}) copy-start(f32[3,128,512]{2,1,0:T(8,128)S(1)} %multiply_add_fusion.3) | copy-start | bytes 2359300
  43.2 6.6 %copy-start.16 = (f32[128,512]{1,0:T(8,128)}, f32[128,512]{1,0:T(8,128)S(1)}, u32[]{:S(2)}) copy-start(f32[128,512]{1,0:T(8,128)S(1)} %get-tuple-element.12) | copy-start | bytes 786436
  43.2 3.2 collective-permute-start.2
  56.0 31.5 %all-to-all-start.2 = ((bf16[64,2,2048]{2,1,0:T(2,128)(2,1)}), bf16[64,2,2048]{2,1,0:T(2,128)(2,1)S(1)}, u32[]{:S(2)}, u32[]{:S(2)}) async-start(bf16[64,2,2048]{2,1,0:T(2,128)(2,1)} %reshape.83), calls=%async_computation.3 | async-start | bytes 1048576 | tf_op jit(solution)/shard_map/all_to_all | solution.py:148
  87.4 0.8 copy-start.13
  88.2 57.2 %all-to-all-start = ((f32[1,256,2048]{2,0,1:T(1,128)}), f32[1,256,2048]{2,0,1:T(1,128)S(1)}, u32[]{:S(2)}, u32[]{:S(2)}) async-start(f32[1,256,2048]{2,0,1:T(1,128)} %copy.39), calls=%async_computation | async-start | bytes 4194304 | tf_op jit(solution)/shard_map/all_to_all | solution.py:106
  160.5 2.4 copy-start.8
  160.6 2.4 copy-start.9
  165.8 3.5 copy-start.4
  172.6 34.3 %all-to-all-start.1 = ((f32[64,4,1024]{2,1,0:T(4,128)}), f32[64,4,1024]{2,1,0:T(4,128)}, u32[]{:S(2)}, u32[]{:S(2)}) async-start(f32[64,4,1024]{2,1,0:T(4,128)} %copy.44), calls=%async_computation.1 | async-start | bytes 2097152 | tf_op jit(solution)/shard_map/all_to_all | solution.py:121
  178.2 1.2 copy-start.3
  178.2 2.8 copy-start.12
  180.2 1.6 copy-start.5
  206.9 34.7 %all-to-all-start.3 = ((bf16[64,4,2048]{2,1,0:T(4,128)(2,1)}), bf16[64,4,2048]{2,1,0:T(4,128)(2,1)S(1)}, u32[]{:S(2)}, u32[]{:S(2)}) async-start(bf16[64,4,2048]{2,1,0:T(4,128)(2,1)} %copy.48), calls=%async_computation.4 | async-start | bytes 2097152 | tf_op jit(solution)/shard_map/all_to_all | solution.py:161
  212.8 68.2 %reduce-scatter.3.cloned.1.call-start = ((), (), s32[]{:S(2)}) async-start(), calls=%async_computation.6 | async-start | bytes 2621440 | tf_op jit(solution)/shard_map/reduce_scatter | solution.py:132
  217.7 0.8 copy-start.14
  217.7 26.8 %copy-start.17 = (f32[128,512]{1,0:T(8,128)S(1)}, f32[128,512]{1,0:T(8,128)}, u32[]{:S(2)}) copy-start(f32[128,512]{1,0:T(8,128)} %copy-done.16) | copy-start | bytes 786436
  217.7 26.8 %copy-start.20 = (f32[512]{0:T(512)S(1)}, f32[512]{0:T(512)}, u32[]{:S(2)}) copy-start(f32[512]{0:T(512)} %param.13) | copy-start | bytes 6148
  218.5 28.0 %copy-start.19 = (f32[128,512]{1,0:T(8,128)S(1)}, f32[128,512]{1,0:T(8,128)}, u32[]{:S(2)}) copy-start(f32[128,512]{1,0:T(8,128)} %get-tuple-element.42) | copy-start | bytes 786436
  218.5 28.0 %collective-permute-start.1 = (f32[128,512]{1,0:T(8,128)S(1)}, f32[128,512]{1,0:T(8,128)}, u32[]{:S(2)}, u32[]{:S(2)}) collective-permute-start(f32[128,512]{1,0:T(8,128)S(1)} %slice.148), channel_id=1, source_target_pairs={{0,4},{4,8},{8,12},{12,16},{16,20},{20,24},{24,28},{28,32},{32,36}... | collective-permute-start | bytes 786440 | tf_op jit(solution)/shard_map/ppermute | solution.py:13
  221.4 25.1 %copy-start.15 = (f32[256,512]{1,0:T(8,128)S(1)}, f32[256,512]{1,0:T(8,128)}, u32[]{:S(2)}) copy-start(f32[256,512]{1,0:T(8,128)} %copy-done.14) | copy-start | bytes 1572868
  242.8 4.8 %copy-start.7 = (f32[3,128,512]{2,1,0:T(8,128)S(1)}, f32[3,128,512]{2,1,0:T(8,128)}, u32[]{:S(2)}) copy-start(f32[3,128,512]{2,1,0:T(8,128)} %copy-done.6) | copy-start | bytes 2359300
  244.5 3.1 copy-start.2
  249.7 1.7 copy-start.10
  249.8 189.7 %reduce-scatter.5.cloned.1.call-start = ((), (), s32[]{:S(2)}) async-start(), calls=%async_computation.8 | async-start | bytes 10649600 | tf_op jit(solution)/shard_map/reduce_scatter | solution.py:204
  250.0 15.1 %collective-permute-start.3 = (f32[3,2,512]{2,1,0:T(2,128)S(1)}, f32[3,2,512]{2,1,0:T(2,128)S(1)}, u32[]{:S(2)}, u32[]{:S(2)}) collective-permute-start(f32[3,2,512]{2,1,0:T(2,128)S(1)} %slice.153), channel_id=1, source_target_pairs={{4,0},{8,4},{12,8},{16,12},{20,16},{24,20},{28,24},{32,28},{36,32}... | collective-permute-start | bytes 36872 | tf_op jit(solution)/shard_map/ppermute | solution.py:13
  276.6 1.2 copy-start.18
  277.9 2.2 copy-start.11
  277.9 165.8 %copy-start.1 = (f32[128,512]{1,0:T(8,128)S(1)}, f32[128,512]{1,0:T(8,128)}, u32[]{:S(2)}) copy-start(f32[128,512]{1,0:T(8,128)} %param.12) | copy-start | bytes 786436
Sparse Core Ops, SparseCore 0:
  9.8 28.5 all-gather.1
  249.9 27.6 reduce-scatter.2
  282.5 156.9 reduce-scatter.4
where the time goes:
time: 460 us; the launch traced here: 451 us
  waiting for transfers between devices  269 us (58%)
  matrix products  54.6 us (12%)
  local copies, waits for them, and re-layouts  46.4 us (10%)
  starting transfers between devices  38.5 us (8%)
  other arithmetic  27.3 us (6%)
  between operations  14.9 us (3%)
    reduce_scatter x1, waiting for transfers between devices, on_device(): lax.psum_scatter(combined.reshape(-1, channel_count), 'seq', scatter_dime...  157 us
    dot_general x36, matrix products, along_rows(): return jnp.tensordot(factor, values, axes=1, precision=exact_mode)  43.2 us
    all_to_all x1, waiting for transfers between devices, on_device(): lax.all_to_all(jnp.concatenate([input_pair[0], input_pair[1], filter_pair...  33.2 us
    all_gather x1, waiting for transfers between devices, on_device(): full_cotangent = lax.all_gather(cotangent, 'ch', axis=1, tiled=True)  25.7 us
    all_to_all x1, waiting for transfers between devices, on_device(): lax.all_to_all(jnp.concatenate(inverse_pair, axis=-1), 'seq', split_axis=...  20.8 us
    all_to_all x1, waiting for transfers between devices, on_device(): lax.all_to_all(as_sent(jnp.concatenate(input_back + filter_back, axis=-1)...  20.3 us
    all_to_all x1, starting transfers between devices, on_device(): lax.all_to_all(jnp.concatenate(grad_pair, axis=1)[None].astype(jnp.bfloat...  13.8 us
    all_to_all x1, waiting for transfers between devices, on_device(): lax.all_to_all(jnp.concatenate(grad_pair, axis=1)[None].astype(jnp.bfloat...  9.73 us
  transfers between devices with their start and end apart: 11, of which 7 were waited for; matrix products, arithmetic and copies ran while one was open for 16% of the time, Pallas kernels for 0%

commit v1 on v0

--- a/solution.py
+++ b/solution.py
@@ -132,7 +132,12 @@
     layer_out = lax.psum_scatter(partial_value, "ch", scatter_dimension=1, tiled=True).astype(
         jnp.bfloat16
     )
-    full_cotangent = lax.all_gather(cotangent, "ch", axis=1, tiled=True)
+    ring = [cotangent]
+    for hop in range(3):
+        ring.append(lax.ppermute(ring[-1], "ch", [(dev, (dev + 1) % 4) for dev in range(4)]))
+    full_cotangent = jnp.roll(
+        jnp.concatenate(ring[::-1], axis=1), (lax.axis_index("ch") + 1) * ring[0].shape[1], axis=1
+    )
     grad_gated = lax.dot_general(
         full_cotangent, out_weight, (((1,), (1,)), ((), ())), preferred_element_type=jnp.float32
     )

time: 460 us -> 446 us (0.970)
  local copies, waits for them, and re-layouts: 46.4 us -> 37.5 us
  starting transfers between devices: 38.5 us -> 44.9 us
  waiting for transfers between devices: 269 us -> 263 us
    all_gather x1 -> x0, waiting for transfers between devices: 25.7 us -> none  [on_device(): full_cotangent = lax.all_gather(cotangent, 'ch', axis=1, tiled=True)]
    ppermute x0 -> x3, waiting for transfers between devices: none -> 12.7 us  [on_device(): lax.ppermute(ring[-1], 'ch', [(dev, (dev + 1) % 4) for dev in range(4)])]
    dot_general x1 -> x0, local copies, waits for them, and re-layouts: 9.14 us -> none  [on_device(): lax.dot_general(full_cotangent, gated_values, (((0,), (0,)), ((), ())), p...]
    ppermute x0 -> x3, starting transfers between devices: none -> 4.84 us  [on_device(): lax.ppermute(ring[-1], 'ch', [(dev, (dev + 1) % 4) for dev in range(4)])]
    unnamed x47 -> x58, local copies, waits for them, and re-layouts: 9.71 us -> 9.94 us
  transfers between devices with their start and end apart: 11 -> 13, of which waited for: 7 -> 10; matrix products, arithmetic and copies ran while one was open for 16% -> 14% of each run, Pallas kernels for 0% -> 0%
where the time goes in v1:
time: 446 us; the launch traced here: 441 us
  waiting for transfers between devices  263 us (59%)
  matrix products  53.3 us (12%)
  starting transfers between devices  44.9 us (10%)
  local copies, waits for them, and re-layouts  37.5 us (8%)
  other arithmetic  27.2 us (6%)
  between operations  15.3 us (3%)
    reduce_scatter x1, waiting for transfers between devices, on_device(): lax.psum_scatter(combined.reshape(-1, channel_count), 'seq', scatter_dime...  160 us
    dot_general x36, matrix products, along_rows(): return jnp.tensordot(factor, values, axes=1, precision=exact_mode)  43.2 us
    all_to_all x1, waiting for transfers between devices, on_device(): lax.all_to_all(jnp.concatenate([input_pair[0], input_pair[1], filter_pair...  33.1 us
    all_to_all x1, waiting for transfers between devices, on_device(): lax.all_to_all(jnp.concatenate(inverse_pair, axis=-1), 'seq', split_axis=...  20.8 us
    all_to_all x1, waiting for transfers between devices, on_device(): lax.all_to_all(as_sent(jnp.concatenate(input_back + filter_back, axis=-1)...  20.2 us
    all_to_all x1, starting transfers between devices, on_device(): lax.all_to_all(jnp.concatenate(grad_pair, axis=1)[None].astype(jnp.bfloat...  15.6 us
    ppermute x3, waiting for transfers between devices, on_device(): lax.ppermute(ring[-1], 'ch', [(dev, (dev + 1) % 4) for dev in range(4)])  12.7 us
    unnamed x58, local copies, waits for them, and re-layouts  9.94 us
  transfers between devices with their start and end apart: 13, of which 10 were waited for; matrix products, arithmetic and copies ran while one was open for 14% of the time, Pallas kernels for 0%

profile of v1, /device:TPU:2, one launch (start us, length us, event | category | flops | bytes accessed | tf_op | source)
XLA Modules:
  0.0 441.0 jit_solution(6348839327995530225)
XLA Ops:
  7.2 1.6 collective-permute-start.2
  9.5 1.5 collective-permute-start
  11.8 3.7 collective-permute-done.2
  15.5 1.5 collective-permute-start.3
  17.0 1.1 maximum_convert_fusion
  18.2 4.2 collective-permute-done.3
  22.4 1.8 collective-permute-start.4
  24.4 4.8 %collective-permute-done.4 = bf16[128,1024]{1,0:T(8,128)(2,1)S(1)} collective-permute-done((bf16[128,1024]{1,0:T(8,128)(2,1)S(1)}, bf16[128,1024]{1,0:T(8,128)(2,1)S(1)}, u32[]{:S(2)}, u32[]{:S(2)}) %collective-permute-start.4) | collective-permute-done | bytes 262176 | tf_op jit(solution)/shard_map/ppermute | solution.py:137
  29.5 2.2 multiply_reduce_fusion.3
  31.8 1.5 collective-permute-start.5
  33.3 1.7 collective-permute-done.5
  35.1 1.6 fusion.12
  36.7 1.6 fusion.13
  39.7 3.7 reduce.3
  43.4 1.1 reshape.83
  44.6 15.6 %all-to-all-start.2 = ((bf16[64,2,2048]{2,1,0:T(2,128)(2,1)}), bf16[64,2,2048]{2,1,0:T(2,128)(2,1)S(1)}, u32[]{:S(2)}, u32[]{:S(2)}) async-start(bf16[64,2,2048]{2,1,0:T(2,128)(2,1)} %reshape.83), calls=%async_computation.3 | async-start | bytes 1048576 | tf_op jit(solution)/shard_map/all_to_all | solution.py:153
  60.2 1.1 convolution_negate_fusion.1
  62.3 1.1 convolution_negate_fusion.2
  64.6 3.5 copy.34
  68.0 9.7 %all-to-all-done.2 = bf16[64,2,2048]{2,1,0:T(2,128)(2,1)S(1)} async-done(((bf16[64,2,2048]{2,1,0:T(2,128)(2,1)}), bf16[64,2,2048]{2,1,0:T(2,128)(2,1)S(1)}, u32[]{:S(2)}, u32[]{:S(2)}) %all-to-all-start.2) | async-done | bytes 524320 | tf_op jit(solution)/shard_map/all_to_all | solution.py:153
  78.6 5.8 %all-to-all-start = ((f32[1,256,2048]{2,0,1:T(1,128)}), f32[1,256,2048]{2,0,1:T(1,128)S(1)}, u32[]{:S(2)}, u32[]{:S(2)}) async-start(f32[1,256,2048]{2,0,1:T(1,128)} %copy.34), calls=%async_computation | async-start | bytes 4194304 | tf_op jit(solution)/shard_map/all_to_all | solution.py:106
  84.4 4.9 %reshape.84 = bf16[256,1,1024]{2,1,0:T(2,128)(2,1)} reshape(bf16[64,2,2048]{2,1,0:T(2,128)(2,1)} %copy-done.14) | data formatting | bytes 1048576
  89.3 5.1 %bitcast_reduce_fusion = bf16[256,1024]{1,0:T(8,128)(2,1)} fusion(bf16[256,1,1024]{2,1,0:T(2,128)(2,1)} %reshape.84), kind=kLoop, calls=%fused_computation.358 | loop fusion | bytes 1048576 | tf_op jit(solution)/shard_map/all_to_all | solution.py:153
  94.4 2.0 all_to_all.41
  96.4 1.2 fusion.307
  99.1 1.7 convolution_add_fusion
  100.9 1.8 convolution_subtract_fusion
  102.6 33.1 %all-to-all-done = f32[1,256,2048]{2,0,1:T(1,128)S(1)} async-done(((f32[1,256,2048]{2,0,1:T(1,128)}), f32[1,256,2048]{2,0,1:T(1,128)S(1)}, u32[]{:S(2)}, u32[]{:S(2)}) %all-to-all-start) | async-done | bytes 2097184 | tf_op jit(solution)/shard_map/all_to_all | solution.py:106
  135.7 6.8 %reduce = f32[256,2048]{1,0:T(8,128)} reduce(f32[1,256,2048]{2,0,1:T(1,128)S(1)} %all-to-all-done, f32[]{:T(128)} %constant.100), dimensions={0}, to_apply=%all_to_all.16.reduce_sub_computation | reduce | bytes 4194308 | tf_op jit(solution)/shard_map/all_to_all | solution.py:106
  142.5 2.0 all_to_all.17
  144.9 1.2 fusion.28
  146.1 1.2 fusion.24
  147.3 1.2 convolution_add_fusion.1
  148.5 1.2 convolution_subtract_fusion.1
  149.7 1.2 fusion.34
  150.9 1.2 fusion.30
  152.1 1.2 convolution_add_fusion.2
  153.3 2.8 multiply_add_fusion.1
  156.1 1.6 fusion.115
  161.2 1.7 copy.39
  162.9 5.6 %all-to-all-start.1 = ((f32[64,4,1024]{2,1,0:T(4,128)}), f32[64,4,1024]{2,1,0:T(4,128)}, u32[]{:S(2)}, u32[]{:S(2)}) async-start(f32[64,4,1024]{2,1,0:T(4,128)} %copy.39), calls=%async_computation.1 | async-start | bytes 2097152 | tf_op jit(solution)/shard_map/all_to_all | solution.py:121
  174.7 1.8 copy.43
  176.4 20.8 %all-to-all-done.1 = f32[64,4,1024]{2,1,0:T(4,128)} async-done(((f32[64,4,1024]{2,1,0:T(4,128)}), f32[64,4,1024]{2,1,0:T(4,128)}, u32[]{:S(2)}, u32[]{:S(2)}) %all-to-all-start.1) | async-done | bytes 1048608 | tf_op jit(solution)/shard_map/all_to_all | solution.py:121
  197.2 5.8 %all-to-all-start.3 = ((bf16[64,4,2048]{2,1,0:T(4,128)(2,1)}), bf16[64,4,2048]{2,1,0:T(4,128)(2,1)S(1)}, u32[]{:S(2)}, u32[]{:S(2)}) async-start(bf16[64,4,2048]{2,1,0:T(4,128)(2,1)} %copy.43), calls=%async_computation.4 | async-start | bytes 2097152 | tf_op jit(solution)/shard_map/all_to_all | solution.py:166
  203.1 1.6 all_to_all.19
  204.7 1.6 fusion.23
  206.3 1.6 fusion.6
  208.7 2.9 collective-permute-start.1
  211.7 20.2 %all-to-all-done.3 = bf16[64,4,2048]{2,1,0:T(4,128)(2,1)S(1)} async-done(((bf16[64,4,2048]{2,1,0:T(4,128)(2,1)}), bf16[64,4,2048]{2,1,0:T(4,128)(2,1)S(1)}, u32[]{:S(2)}, u32[]{:S(2)}) %all-to-all-start.3) | async-done | bytes 1048608 | tf_op jit(solution)/shard_map/all_to_all | solution.py:166
  231.9 1.1 all_to_all.43
  233.0 1.8 fusion.40
  234.8 1.9 fusion.16
  237.9 2.1 fusion.309
  240.2 1.3 collective-permute-start.6
  241.5 5.8 %fusion.17 = f32[4096,512]{1,0:T(8,128)} fusion(bf16[128,512]{1,0:T(8,128)(2,1)S(1)} %get-tuple-element.36, bf16[128,8192]{1,0:T(8,128)(2,1)} %copy-done.12, s32[]{:T(128)S(6)} %select_n.110), kind=kOutput, calls=%fused_computation.46 | convolution fusion | flops 536870912 | bytes 9568260 | tf_op jit(solution)/shard_map/dot_general | solution.py:144
  247.4 1.4 multiply_reduce_fusion.2
  249.2 9.6 %pad_maximum_fusion = f32[64,80,512]{2,1,0:T(8,128)} fusion(f32[64,16,512]{2,1,0:T(8,128)S(1)} %broadcast_in_dim.18, f32[64,64,512]{2,1,0:T(8,128)} %bitcast.150), kind=kLoop, calls=%fused_computation | loop fusion | flops 2621440 | bytes 20971520 | tf_op jit(solution)/shard_map/concatenate | solution.py:205
  258.8 1.2 copy-done.19
  260.8 1.5 fusion.14
  263.2 4.5 %reduce-scatter.3.cloned.1.call-done = f32[128,1024]{1,0:T(8,128)} async-done(((f32[128,4096]{1,0:T(8,128)}), f32[128,1024]{1,0:T(8,128)}) %reduce-scatter.3.cloned.1.call-update) | async-done | bytes 524304 | tf_op jit(solution)/shard_map/reduce_scatter | solution.py:132
  267.7 1.8 convert_element_type.109
  269.4 160.1 %reduce-scatter.5.cloned.1.call-done = f32[80,512]{1,0:T(8,128)} async-done(((f32[5120,512]{1,0:T(8,128)}), f32[80,512]{1,0:T(8,128)}) %reduce-scatter.5.cloned.1.call-update) | async-done | bytes 163856 | tf_op jit(solution)/shard_map/reduce_scatter | solution.py:209
  430.9 1.6 slice.163
  432.5 1.3 slice.162
  (108 shorter events, 23.7 us)
Async XLA Ops:
  7.2 53.0 %copy-start = (f32[128,512]{1,0:T(8,128)S(1)}, f32[128,512]{1,0:T(8,128)}, u32[]{:S(2)}) copy-start(f32[128,512]{1,0:T(8,128)} %param.12) | copy-start | bytes 786436
  7.2 8.3 %collective-permute-start.2 = (bf16[128,1024]{1,0:T(8,128)(2,1)}, bf16[128,1024]{1,0:T(8,128)(2,1)S(1)}, u32[]{:S(2)}, u32[]{:S(2)}) collective-permute-start(bf16[128,1024]{1,0:T(8,128)(2,1)} %param.15), channel_id=1, source_target_pairs={{0,1},{1,2},{2,3},{3,0},{4,5},{5,6},{6,7},{7,4},{8,9},{9,10},{10,1... | collective-permute-start | bytes 786440 | tf_op jit(solution)/shard_map/ppermute | solution.py:137
  9.5 7.5 %collective-permute-start = (bf16[3,2,512]{2,1,0:T(2,128)(2,1)S(1)}, bf16[3,2,512]{2,1,0:T(2,128)(2,1)S(1)}, u32[]{:S(2)}, u32[]{:S(2)}) collective-permute-start(bf16[3,2,512]{2,1,0:T(2,128)(2,1)S(1)} %pad_maximum_fusion.10), channel_id=1, source_target_pairs={{0,4},{4,8},{8,12},{12,16},{16,20},{20,24},{24,28},{28,32},{32,36}... | collective-permute-start | bytes 18440 | tf_op jit(solution)/shard_map/ppermute | solution.py:13
  15.5 6.9 %collective-permute-start.3 = (bf16[128,1024]{1,0:T(8,128)(2,1)S(1)}, bf16[128,1024]{1,0:T(8,128)(2,1)S(1)}, u32[]{:S(2)}, u32[]{:S(2)}) collective-permute-start(bf16[128,1024]{1,0:T(8,128)(2,1)S(1)} %collective-permute-done.2), channel_id=1, source_target_pairs={{0,1},{1,2},{2,3},{3,0},{4,5},{5,6},{6,7},{7,4},{8,9},{9,10},{10,1... | collective-permute-start | bytes 786440 | tf_op jit(solution)/shard_map/ppermute | solution.py:137
  22.4 6.9 %collective-permute-start.4 = (bf16[128,1024]{1,0:T(8,128)(2,1)S(1)}, bf16[128,1024]{1,0:T(8,128)(2,1)S(1)}, u32[]{:S(2)}, u32[]{:S(2)}) collective-permute-start(bf16[128,1024]{1,0:T(8,128)(2,1)S(1)} %collective-permute-done.3), channel_id=1, source_target_pairs={{0,1},{1,2},{2,3},{3,0},{4,5},{5,6},{6,7},{7,4},{8,9},{9,10},{10,1... | collective-permute-start | bytes 786440 | tf_op jit(solution)/shard_map/ppermute | solution.py:137
  24.2 5.2 %copy-start.20 = (bf16[128,1024]{1,0:T(8,128)(2,1)S(1)}, bf16[128,1024]{1,0:T(8,128)(2,1)}, u32[]{:S(2)}) copy-start(bf16[128,1024]{1,0:T(8,128)(2,1)} %param.15) | copy-start | bytes 786436
  24.2 5.3 %copy-start.2 = (bf16[512,4096]{1,0:T(8,128)(2,1)S(1)}, bf16[512,4096]{1,0:T(8,128)(2,1)}, u32[]{:S(2)}) copy-start(bf16[512,4096]{1,0:T(8,128)(2,1)} %param.14) | copy-start | bytes 12582916
  24.4 5.1 %copy-start.7 = (f32[3,128,512]{2,1,0:T(8,128)}, f32[3,128,512]{2,1,0:T(8,128)S(1)}, u32[]{:S(2)}) copy-start(f32[3,128,512]{2,1,0:T(8,128)S(1)} %multiply_add_fusion.3) | copy-start | bytes 2359300
  29.5 2.3 copy-start.12
  31.8 6.6 %copy-start.17 = (f32[128,512]{1,0:T(8,128)}, f32[128,512]{1,0:T(8,128)S(1)}, u32[]{:S(2)}) copy-start(f32[128,512]{1,0:T(8,128)S(1)} %get-tuple-element.12) | copy-start | bytes 786436
  31.8 3.2 collective-permute-start.5
  44.6 33.2 %all-to-all-start.2 = ((bf16[64,2,2048]{2,1,0:T(2,128)(2,1)}), bf16[64,2,2048]{2,1,0:T(2,128)(2,1)S(1)}, u32[]{:S(2)}, u32[]{:S(2)}) async-start(bf16[64,2,2048]{2,1,0:T(2,128)(2,1)} %reshape.83), calls=%async_computation.3 | async-start | bytes 1048576 | tf_op jit(solution)/shard_map/all_to_all | solution.py:153
  77.8 0.8 copy-start.14
  78.6 57.2 %all-to-all-start = ((f32[1,256,2048]{2,0,1:T(1,128)}), f32[1,256,2048]{2,0,1:T(1,128)S(1)}, u32[]{:S(2)}, u32[]{:S(2)}) async-start(f32[1,256,2048]{2,0,1:T(1,128)} %copy.34), calls=%async_computation | async-start | bytes 4194304 | tf_op jit(solution)/shard_map/all_to_all | solution.py:106
  150.9 2.4 copy-start.9
  150.9 2.4 copy-start.10
  156.1 3.4 copy-start.5
  162.9 34.3 %all-to-all-start.1 = ((f32[64,4,1024]{2,1,0:T(4,128)}), f32[64,4,1024]{2,1,0:T(4,128)}, u32[]{:S(2)}, u32[]{:S(2)}) async-start(f32[64,4,1024]{2,1,0:T(4,128)} %copy.39), calls=%async_computation.1 | async-start | bytes 2097152 | tf_op jit(solution)/shard_map/all_to_all | solution.py:121
  168.5 1.2 copy-start.4
  168.5 2.8 copy-start.13
  170.5 1.6 copy-start.6
  197.2 34.7 %all-to-all-start.3 = ((bf16[64,4,2048]{2,1,0:T(4,128)(2,1)}), bf16[64,4,2048]{2,1,0:T(4,128)(2,1)S(1)}, u32[]{:S(2)}, u32[]{:S(2)}) async-start(bf16[64,4,2048]{2,1,0:T(4,128)(2,1)} %copy.43), calls=%async_computation.4 | async-start | bytes 2097152 | tf_op jit(solution)/shard_map/all_to_all | solution.py:166
  203.0 64.6 %reduce-scatter.3.cloned.1.call-start = ((), (), s32[]{:S(2)}) async-start(), calls=%async_computation.6 | async-start | bytes 2621440 | tf_op jit(solution)/shard_map/reduce_scatter | solution.py:132
  207.9 0.8 copy-start.15
  207.9 26.8 %copy-start.18 = (f32[128,512]{1,0:T(8,128)S(1)}, f32[128,512]{1,0:T(8,128)}, u32[]{:S(2)}) copy-start(f32[128,512]{1,0:T(8,128)} %copy-done.17) | copy-start | bytes 786436
  208.0 26.8 %copy-start.22 = (f32[512]{0:T(512)S(1)}, f32[512]{0:T(512)}, u32[]{:S(2)}) copy-start(f32[512]{0:T(512)} %param.13) | copy-start | bytes 6148
  208.7 28.0 %copy-start.21 = (f32[128,512]{1,0:T(8,128)S(1)}, f32[128,512]{1,0:T(8,128)}, u32[]{:S(2)}) copy-start(f32[128,512]{1,0:T(8,128)} %get-tuple-element.42) | copy-start | bytes 786436
  208.7 28.0 %collective-permute-start.1 = (f32[128,512]{1,0:T(8,128)S(1)}, f32[128,512]{1,0:T(8,128)}, u32[]{:S(2)}, u32[]{:S(2)}) collective-permute-start(f32[128,512]{1,0:T(8,128)S(1)} %slice.148), channel_id=1, source_target_pairs={{0,4},{4,8},{8,12},{12,16},{16,20},{20,24},{24,28},{28,32},{32,36}... | collective-permute-start | bytes 786440 | tf_op jit(solution)/shard_map/ppermute | solution.py:13
  211.7 25.1 %copy-start.16 = (f32[256,512]{1,0:T(8,128)S(1)}, f32[256,512]{1,0:T(8,128)}, u32[]{:S(2)}) copy-start(f32[256,512]{1,0:T(8,128)} %copy-done.15) | copy-start | bytes 1572868
  233.0 4.8 %copy-start.8 = (f32[3,128,512]{2,1,0:T(8,128)S(1)}, f32[3,128,512]{2,1,0:T(8,128)}, u32[]{:S(2)}) copy-start(f32[3,128,512]{2,1,0:T(8,128)} %copy-done.7) | copy-start | bytes 2359300
  234.8 3.1 copy-start.3
  240.0 189.5 %reduce-scatter.5.cloned.1.call-start = ((), (), s32[]{:S(2)}) async-start(), calls=%async_computation.7 | async-start | bytes 10649600 | tf_op jit(solution)/shard_map/reduce_scatter | solution.py:209
  240.2 7.1 %collective-permute-start.6 = (f32[3,2,512]{2,1,0:T(2,128)S(1)}, f32[3,2,512]{2,1,0:T(2,128)S(1)}, u32[]{:S(2)}, u32[]{:S(2)}) collective-permute-start(f32[3,2,512]{2,1,0:T(2,128)S(1)} %slice.153), channel_id=1, source_target_pairs={{4,0},{8,4},{12,8},{16,12},{20,16},{24,20},{28,24},{32,28},{36,32}... | collective-permute-start | bytes 36872 | tf_op jit(solution)/shard_map/ppermute | solution.py:13
  258.8 1.2 copy-start.19
  260.0 2.2 copy-start.11
  260.0 173.7 %copy-start.1 = (f32[128,512]{1,0:T(8,128)S(1)}, f32[128,512]{1,0:T(8,128)}, u32[]{:S(2)}) copy-start(f32[128,512]{1,0:T(8,128)} %param.12) | copy-start | bytes 786436
Sparse Core Ops, SparseCore 0:
  240.1 27.4 reduce-scatter.2
  272.5 156.9 reduce-scatter.4
